TPU v7x, 256 devices: a whole 4x4x8 slice. The times are simulated.
256 devices in a mesh: grp: 4 (over y), dev: 64 (over x, z, core).
Axes of the slice: x: 4, y: 4, z: 8, core: 2. Of those that a mesh axis runs over, the one named last changes fastest.
Arguments:
- field: float32 [512, 512, 256, 4], P('dev', 'grp'), may hold values from -21 to 21
- start_basis: float32 [512, 64], replicated, may hold values from -6 to 6
Outputs:
- factor: float32 [512, 64], replicated
- core: float32 [64, 512, 256, 4], P(None, ('grp', 'dev'))
All inputs are finite; a program needn't handle non-finite values.
Results may differ from a plain program's by a relative error of at most 0.0003.
Values sent between devices are 32-bit elements; how exact they have to be, the bound alone decides.
No kernel may reach another device: no remote copies, remote signals or barrier semaphores. Data moves between devices by JAX's collectives and lax.ppermute only.
A program may use at most 192 MiB of HBM per device.

v0:
```python
import jax
import jax.numpy as jnp
from jax import lax
from jax.sharding import PartitionSpec as P

ITERS = 3


def product(left, right):
    return jnp.dot(left, right, precision=lax.Precision.HIGHEST, preferred_element_type=jnp.float32)


def on_device(field, start_basis):
    regrouped = lax.all_to_all(field, "dev", split_axis=1, concat_axis=0, tiled=True)
    rows = regrouped.shape[0]
    local_cols = regrouped.shape[1] * regrouped.shape[2] * regrouped.shape[3]
    unfold = regrouped.reshape(rows, local_cols)
    local_gram = product(unfold, unfold.T)
    gram = lax.psum(local_gram, ("grp", "dev"))
    basis = start_basis
    for step in range(ITERS):
        image = product(gram, basis)
        cross = product(image.T, image)
        chol = jnp.linalg.cholesky(cross)
        basis = lax.linalg.triangular_solve(
            chol, image, left_side=False, lower=True, transpose_a=True
        )
    core = product(basis.T, unfold)
    return (
        basis,
        core.reshape(basis.shape[1], regrouped.shape[1], regrouped.shape[2], regrouped.shape[3]),
    )


def solution(mesh):
    placed = (P("dev", "grp", None, None), P())
    return jax.shard_map(
        on_device,
        mesh=mesh,
        in_specs=placed,
        out_specs=(P(), P(None, ("grp", "dev"), None, None)),
        check_vma=False,
    )
```

profile of v0, /device:TPU:2, one launch (start us, length us, event | category | flops | bytes accessed | tf_op | source)
XLA Modules:
  0.0 543.9 jit_solution(3584140676412488919)
XLA Ops:
  7.2 0.0 copy-start
  7.2 0.0 all-reduce.2.cloned.1.call-start
  7.2 3.4 copy.14
  10.7 106.2 %all_to_all.15 = f32[8,128,256,4]{2,3,0,1:T(4,128)} all-to-all(f32[8,128,256,4]{2,3,0,1:T(4,128)S(1)} %copy.14), channel_id=1, replica_groups=mesh['grp'=4,'dev'=64] {'dev'}, dimensions={1} | all-to-all | bytes 8388608 | tf_op jit(solution)/shard_map/all_to_all | solution.py:14
  116.9 50.4 %copy.15 = f32[8,64,2,256,4]{0,1,4,3,2:T(8,128)} copy(f32[8,64,2,256,4]{3,4,0,2,1:T(4,128)} %bitcast.63) | data formatting | bytes 8388608 | tf_op jit(solution)/shard_map/all_to_all | solution.py:14
  167.2 48.3 %reshape.21 = f32[512,2048]{0,1:T(8,128)} reshape(f32[64,8,2,256,4]{1,0,4,3,2:T(8,128)} %bitcast.1) | data formatting | bytes 8388608 | tf_op jit(solution)/shard_map/reshape | solution.py:17
  215.5 11.3 %fusion.17 = f32[512,512]{1,0:T(8,128)} fusion(f32[512,2048]{0,1:T(8,128)} %reshape.21), kind=kOutput, calls=%fused_computation.31 | convolution fusion | flops 6442450944 | bytes 5242880 | tf_op jit(solution)/shard_map/dot_general | solution.py:10
  226.9 0.0 all-reduce.2.cloned.1.call-update
  226.9 5.2 dot_general.36
  232.1 252.3 %all-reduce.2.cloned.1.call-done = f32[512,512]{1,0:T(8,128)} async-done(((f32[512,512]{1,0:T(8,128)}), f32[512,512]{1,0:T(8,128)}) %all-reduce.2.cloned.1.call-update) | async-done | bytes 1048592 | tf_op jit(solution)/shard_map/psum | solution.py:19
  484.4 0.0 copy-done
  484.4 0.0 copy-start.1
  484.4 2.4 fusion.18
  486.9 0.3 fusion.19
  487.2 0.1 copy.16
  487.2 5.8 %cholesky.59 = f32[64,64]{1,0:T(8,128)S(1)} custom-call(f32[64,64]{1,0:T(8,128)S(1)} %fusion.12), custom_call_target="Cholesky" | custom-call | tf_op jit(solution)/shard_map/jit(cholesky)/cholesky | solution.py:24
  493.1 0.6 compare_reduce_fusion.2
  493.8 0.7 fusion.3
  494.4 4.9 custom-call.7
  499.3 0.3 convolution_bitcast_fusion.1
  499.7 2.4 fusion.20
  502.0 0.3 fusion.21
  502.3 0.1 copy.17
  502.4 5.8 %cholesky.70 = f32[64,64]{1,0:T(8,128)S(1)} custom-call(f32[64,64]{1,0:T(8,128)S(1)} %fusion.10), custom_call_target="Cholesky" | custom-call | tf_op jit(solution)/shard_map/jit(cholesky)/cholesky | solution.py:24
  508.3 0.6 compare_reduce_fusion.1
  508.9 0.7 fusion.4
  509.6 4.9 custom-call.8
  514.5 0.3 convolution_bitcast_fusion
  514.8 0.0 copy-done.1
  514.8 1.1 fusion.22
  516.0 0.3 fusion.23
  516.2 0.1 copy.18
  516.3 5.8 %cholesky.81 = f32[64,64]{1,0:T(8,128)S(1)} custom-call(f32[64,64]{1,0:T(8,128)S(1)} %fusion.8), custom_call_target="Cholesky" | custom-call | tf_op jit(solution)/shard_map/jit(cholesky)/cholesky | solution.py:24
  522.2 0.6 compare_reduce_fusion
  522.9 0.7 fusion.5
  523.5 4.9 custom-call.9
  528.4 0.3 fusion.6
  528.8 0.0 copy-start.2
  528.8 7.1 %fusion = f32[64,2,256,4]{2,0,3,1:T(8,128)S(1)} fusion(f32[2,256,4,512]{3,2,1,0:T(4,128)} %dot_general.36, f32[64,512]{1,0:T(8,128)S(1)} %fusion.6), kind=kOutput, calls=%fused_computation | convolution fusion | flops 805306368 | bytes 4849664 | tf_op jit(solution)/shard_map/dot_general | solution.py:10
  535.9 1.1 copy.20
  537.0 0.0 copy-done.2
  (6 shorter events, 0.1 us)
Async XLA Ops:
  7.2 477.3 %copy-start = (f32[512,64]{0,1:T(8,128)S(1)}, f32[512,64]{0,1:T(8,128)}, u32[]{:S(2)}) copy-start(f32[512,64]{0,1:T(8,128)} %param.6) | copy-start | bytes 393220
  7.2 477.3 %all-reduce.2.cloned.1.call-start = ((), (), s32[]{:S(2)}) async-start(), calls=%async_computation.1 | async-start | bytes 2097152 | tf_op jit(solution)/shard_map/psum | solution.py:19
  484.4 30.4 %copy-start.1 = (f32[512,512]{1,0:T(8,128)S(1)}, f32[512,512]{1,0:T(8,128)}, u32[]{:S(2)}) copy-start(f32[512,512]{1,0:T(8,128)} %all-reduce.2.cloned.1.call-done) | copy-start | bytes 3145732
  528.8 8.3 %copy-start.2 = (f32[64,512]{1,0:T(8,128)}, f32[64,512]{1,0:T(8,128)S(1)}, u32[]{:S(2)}) copy-start(f32[64,512]{1,0:T(8,128)S(1)} %fusion.6) | copy-start | bytes 393220
Sparse Core Ops, SparseCore 0:
  227.0 257.3 all-reduce.1
where the time goes:
time: 545 us; the launch traced here: 544 us
  waiting for transfers between devices  252 us (46%)
  local copies, waits for them, and re-layouts  109 us (20%)
  blocking collectives  106 us (19%)
  other arithmetic  36.2 us (7%)
  matrix products  26.2 us (5%)
  between operations  14.2 us (3%)
    psum x1, waiting for transfers between devices, on_device(): gram = lax.psum(local_gram, ('grp', 'dev'))  252 us
    all_to_all x1, blocking collectives, on_device(): lax.all_to_all(field, 'dev', split_axis=1, concat_axis=0, tiled=True)  106 us
    all_to_all x1, local copies, waits for them, and re-layouts, on_device(): lax.all_to_all(field, 'dev', split_axis=1, concat_axis=0, tiled=True)  50.4 us
    reshape x1, local copies, waits for them, and re-layouts, on_device(): unfold = regrouped.reshape(rows, local_cols)  48.3 us
    dot_general x8, matrix products, product(): jnp.dot(left, right, precision=lax.Precision.HIGHEST, preferred_element_t...  25.2 us
    another operation x9, other arithmetic, on_device(): chol = jnp.linalg.cholesky(cross)  19.6 us
    another operation x6, other arithmetic, on_device(): lax.linalg.triangular_solve(chol, image, left_side=False, lower=True, tra...  16.6 us
  transfers between devices with their start and end apart: 1, of which 1 were waited for; matrix products, arithmetic and copies ran while one was open for 1% of the time, Pallas kernels for 0%

commit v1 on v0

--- a/solution.py
+++ b/solution.py
@@ -16,7 +16,7 @@
     local_cols = regrouped.shape[1] * regrouped.shape[2] * regrouped.shape[3]
     unfold = regrouped.reshape(rows, local_cols)
     local_gram = product(unfold, unfold.T)
-    gram = lax.psum(local_gram, ("grp", "dev"))
+    gram = lax.psum(lax.psum(local_gram, "grp"), "dev")
     basis = start_basis
     for step in range(ITERS):
         image = product(gram, basis)

time: 545 us -> 529 us (0.971)
  waiting for transfers between devices: 252 us -> 236 us
    psum x1 -> x2, waiting for transfers between devices: 252 us -> 236 us  [on_device(): gram = lax.psum(lax.psum(local_gram, 'grp'), 'dev')]
  transfers between devices with their start and end apart: 1 -> 2, of which waited for: 1 -> 2; matrix products, arithmetic and copies ran while one was open for 1% -> 1% of each run, Pallas kernels for 0% -> 0%
where the time goes in v1:
time: 529 us; the launch traced here: 527 us
  waiting for transfers between devices  236 us (45%)
  local copies, waits for them, and re-layouts  109 us (21%)
  blocking collectives  106 us (20%)
  other arithmetic  36.2 us (7%)
  matrix products  26.1 us (5%)
  between operations  14.2 us (3%)
    psum x2, waiting for transfers between devices, on_device(): gram = lax.psum(lax.psum(local_gram, 'grp'), 'dev')  236 us
    all_to_all x1, blocking collectives, on_device(): lax.all_to_all(field, 'dev', split_axis=1, concat_axis=0, tiled=True)  106 us
    all_to_all x1, local copies, waits for them, and re-layouts, on_device(): lax.all_to_all(field, 'dev', split_axis=1, concat_axis=0, tiled=True)  50.4 us
    reshape x1, local copies, waits for them, and re-layouts, on_device(): unfold = regrouped.reshape(rows, local_cols)  48.3 us
    dot_general x8, matrix products, product(): jnp.dot(left, right, precision=lax.Precision.HIGHEST, preferred_element_t...  25.1 us
    another operation x9, other arithmetic, on_device(): chol = jnp.linalg.cholesky(cross)  19.6 us
    another operation x6, other arithmetic, on_device(): lax.linalg.triangular_solve(chol, image, left_side=False, lower=True, tra...  16.6 us
  transfers between devices with their start and end apart: 2, of which 2 were waited for; matrix products, arithmetic and copies ran while one was open for 1% of the time, Pallas kernels for 0%

profile of v1, /device:TPU:2, one launch (start us, length us, event | category | flops | bytes accessed | tf_op | source)
XLA Modules:
  0.0 527.5 jit_solution(3021086049878920090)
XLA Ops:
  7.2 0.0 copy-start
  7.2 0.0 all-reduce.3.cloned.1.call-start
  7.2 3.4 copy.14
  10.7 106.2 %all_to_all.15 = f32[8,128,256,4]{2,3,0,1:T(4,128)} all-to-all(f32[8,128,256,4]{2,3,0,1:T(4,128)S(1)} %copy.14), channel_id=1, replica_groups=mesh['grp'=4,'dev'=64] {'dev'}, dimensions={1} | all-to-all | bytes 8388608 | tf_op jit(solution)/shard_map/all_to_all | solution.py:14
  116.9 50.4 %copy.15 = f32[8,64,2,256,4]{0,1,4,3,2:T(8,128)} copy(f32[8,64,2,256,4]{3,4,0,2,1:T(4,128)} %bitcast.63) | data formatting | bytes 8388608 | tf_op jit(solution)/shard_map/all_to_all | solution.py:14
  167.2 48.3 %reshape.21 = f32[512,2048]{0,1:T(8,128)} reshape(f32[64,8,2,256,4]{1,0,4,3,2:T(8,128)} %bitcast.1) | data formatting | bytes 8388608 | tf_op jit(solution)/shard_map/reshape | solution.py:17
  215.5 11.3 %fusion.17 = f32[512,512]{1,0:T(8,128)} fusion(f32[512,2048]{0,1:T(8,128)} %reshape.21), kind=kOutput, calls=%fused_computation.31 | convolution fusion | flops 6442450944 | bytes 5242880 | tf_op jit(solution)/shard_map/dot_general | solution.py:10
  226.9 0.0 all-reduce.3.cloned.1.call-update
  226.9 0.0 all-reduce.5.cloned.1.call-start
  226.9 49.9 %all-reduce.3.cloned.1.call-done = f32[512,512]{1,0:T(8,128)} async-done(((f32[512,512]{1,0:T(8,128)}), f32[512,512]{1,0:T(8,128)}) %all-reduce.3.cloned.1.call-update) | async-done | bytes 1048592 | tf_op jit(solution)/shard_map/psum | solution.py:19
  276.8 0.0 all-reduce.5.cloned.1.call-update
  276.9 5.2 dot_general.36
  282.0 186.0 %all-reduce.5.cloned.1.call-done = f32[512,512]{1,0:T(8,128)} async-done(((f32[512,512]{1,0:T(8,128)}), f32[512,512]{1,0:T(8,128)}) %all-reduce.5.cloned.1.call-update) | async-done | bytes 1048592 | tf_op jit(solution)/shard_map/psum | solution.py:19
  468.1 0.0 copy-done
  468.1 0.0 copy-start.1
  468.1 2.4 fusion.18
  470.5 0.3 fusion.19
  470.8 0.1 copy.16
  470.9 5.8 %cholesky.59 = f32[64,64]{1,0:T(8,128)S(1)} custom-call(f32[64,64]{1,0:T(8,128)S(1)} %fusion.12), custom_call_target="Cholesky" | custom-call | tf_op jit(solution)/shard_map/jit(cholesky)/cholesky | solution.py:24
  476.8 0.6 compare_reduce_fusion.2
  477.4 0.7 fusion.3
  478.1 4.9 custom-call.7
  483.0 0.3 convolution_bitcast_fusion.1
  483.3 2.4 fusion.20
  485.7 0.3 fusion.21
  485.9 0.1 copy.17
  486.0 5.8 %cholesky.70 = f32[64,64]{1,0:T(8,128)S(1)} custom-call(f32[64,64]{1,0:T(8,128)S(1)} %fusion.10), custom_call_target="Cholesky" | custom-call | tf_op jit(solution)/shard_map/jit(cholesky)/cholesky | solution.py:24
  491.9 0.6 compare_reduce_fusion.1
  492.5 0.7 fusion.4
  493.2 4.9 custom-call.8
  498.1 0.3 convolution_bitcast_fusion
  498.4 0.0 copy-done.1
  498.5 1.1 fusion.22
  499.6 0.3 fusion.23
  499.9 0.1 copy.18
  500.0 5.8 %cholesky.81 = f32[64,64]{1,0:T(8,128)S(1)} custom-call(f32[64,64]{1,0:T(8,128)S(1)} %fusion.8), custom_call_target="Cholesky" | custom-call | tf_op jit(solution)/shard_map/jit(cholesky)/cholesky | solution.py:24
  505.8 0.6 compare_reduce_fusion
  506.5 0.7 fusion.5
  507.1 4.9 custom-call.9
  512.0 0.3 fusion.6
  512.4 0.0 copy-start.2
  512.4 7.1 %fusion = f32[64,2,256,4]{2,0,3,1:T(8,128)S(1)} fusion(f32[2,256,4,512]{3,2,1,0:T(4,128)} %dot_general.36, f32[64,512]{1,0:T(8,128)S(1)} %fusion.6), kind=kOutput, calls=%fused_computation | convolution fusion | flops 805306368 | bytes 4849664 | tf_op jit(solution)/shard_map/dot_general | solution.py:10
  519.5 1.1 copy.20
  520.6 0.0 copy-done.2
  (6 shorter events, 0.1 us)
Async XLA Ops:
  7.2 460.9 %copy-start = (f32[512,64]{0,1:T(8,128)S(1)}, f32[512,64]{0,1:T(8,128)}, u32[]{:S(2)}) copy-start(f32[512,64]{0,1:T(8,128)} %param.6) | copy-start | bytes 393220
  7.2 269.7 %all-reduce.3.cloned.1.call-start = ((), (), s32[]{:S(2)}) async-start(), calls=%async_computation.1 | async-start | bytes 2097152 | tf_op jit(solution)/shard_map/psum | solution.py:19
  226.9 241.2 %all-reduce.5.cloned.1.call-start = ((), (), s32[]{:S(2)}) async-start(), calls=%async_computation.2 | async-start | bytes 2097152 | tf_op jit(solution)/shard_map/psum | solution.py:19
  468.1 30.4 %copy-start.1 = (f32[512,512]{1,0:T(8,128)S(1)}, f32[512,512]{1,0:T(8,128)}, u32[]{:S(2)}) copy-start(f32[512,512]{1,0:T(8,128)} %all-reduce.5.cloned.1.call-done) | copy-start | bytes 3145732
  512.4 8.3 %copy-start.2 = (f32[64,512]{1,0:T(8,128)}, f32[64,512]{1,0:T(8,128)S(1)}, u32[]{:S(2)}) copy-start(f32[64,512]{1,0:T(8,128)S(1)} %fusion.6) | copy-start | bytes 393220
Sparse Core Ops, SparseCore 0:
  227.0 49.7 all-reduce.2
  280.3 187.7 all-reduce.4
